TPU v7x, 128 devices: a whole 4x4x4 slice. The times are simulated.
128 devices in a mesh: row: 8 (over z, x_hi), col: 16 (over y, x_lo, core).
Axes of the slice: x: 4 (x_hi: 2, x_lo: 2; x = x_hi * 2 + x_lo), y: 4, z: 4, core: 2. Of those that a mesh axis runs over, the one named last changes fastest.
Arguments:
- features: bfloat16 [32768, 512], P('row'), may hold values from -6 to 6
- logits: float32 [32768, 128], P(('row', 'col')), may hold values from -16 to 16
Outputs:
- memberships: float32 [32768, 128], P(('row', 'col'))
- standardized: float32 [32768, 128], P(('row', 'col'))
All inputs are finite; a program needn't handle non-finite values.
Results may differ from a plain program's by a relative error of at most 0.0003.
Values may be sent and summed in bfloat16 or wider, within the bound.
A program may use at most 64 MiB of HBM per device.

v0:
```python
import math
import jax
import jax.numpy as jnp
from jax import lax
from jax.sharding import PartitionSpec as P

ITERS = 2


def kernel_product(left_rows, right_rows, members):
    count = left_rows.shape[0]
    feature_width = left_rows.shape[1]
    block_rows = math.gcd(count, 512)
    blocks = left_rows.reshape(count // block_rows, block_rows, feature_width)

    def block_product(block):
        inner = jnp.einsum("bf,nf->bn", block, right_rows, preferred_element_type=jnp.float32)
        base = 1.0 + inner / feature_width
        kernel = base * base * base
        return jnp.dot(
            kernel, members, precision=lax.Precision.HIGHEST, preferred_element_type=jnp.float32
        )

    return lax.map(block_product, blocks).reshape(count, members.shape[1])


def on_device(features, logits):
    frames = logits.shape[0]
    column = lax.axis_index("col")
    own_rows = lax.dynamic_slice_in_dim(features, column * frames, frames, 0)
    column_panel = lax.all_gather(own_rows, "row", axis=0, tiled=True)
    raised = jnp.exp(logits)
    members = raised / jnp.sum(raised, axis=1, keepdims=True)
    standardized = members
    for iteration in range(ITERS):
        members_column = lax.all_gather(members, "row", axis=0, tiled=True)
        scores = lax.psum_scatter(
            kernel_product(features, column_panel, members_column),
            "col",
            scatter_dimension=0,
            tiled=True,
        )
        cluster_size, weighted = lax.psum(
            (jnp.sum(members, axis=0), jnp.sum(members * scores, axis=0)), ("row", "col")
        )
        compact = weighted / (cluster_size * cluster_size)
        distance = compact[None, :] - 2.0 * scores / cluster_size[None, :]
        centered = distance - jnp.mean(distance, axis=1, keepdims=True)
        spread = jnp.mean(centered * centered, axis=1, keepdims=True)
        standardized = centered / jnp.sqrt(spread + 1e-06)
        raised = jnp.exp(-2.0 * standardized)
        members = raised / jnp.sum(raised, axis=1, keepdims=True)
    return (members, standardized)


def solution(mesh):
    return jax.shard_map(
        on_device,
        mesh=mesh,
        in_specs=(P("row", None), P(("row", "col"), None)),
        out_specs=(P(("row", "col"), None), P(("row", "col"), None)),
        check_vma=False,
    )
```

profile of v0, /device:TPU:1, one launch (start us, length us, event | category | flops | bytes accessed | tf_op | source)
XLA Modules:
  0.0 545.2 jit_solution(2299477837792060629)
XLA Ops:
  8.2 1.7 exponential_divide_fusion
  10.0 1.7 constant_dynamic-slice_fusion
  11.7 47.2 %all-gather.6.cloned.1.call-done = f32[2048,128]{1,0:T(8,128)} async-done(((f32[256,128]{1,0:T(8,128)}), f32[2048,128]{1,0:T(8,128)}) %all-gather.6.cloned.1.call-update) | async-done | bytes 1048592 | tf_op jit(solution)/shard_map/all_gather | solution.py:36
  59.0 55.7 %all-gather.4.cloned.1.call-done = bf16[2048,512]{1,0:T(8,128)(2,1)} async-done(((bf16[256,512]{1,0:T(8,128)(2,1)}), bf16[2048,512]{1,0:T(8,128)(2,1)}) %all-gather.4.cloned.1.call-update) | async-done | bytes 2097168 | tf_op jit(solution)/shard_map/all_gather | solution.py:31
  114.8 54.8 %while.20 = (s32[]{:T(128)}, f32[8,512,128]{2,1,0:T(8,128)S(1)}, bf16[8,512,512]{2,1,0:T(8,128)(2,1)}, bf16[2048,512]{1,0:T(8,128)(2,1)}, f32[2048,128]{1,0:T(8,128)}, /*index=5*/s32[]{:T(128)}) while((s32[]{:T(128)}, f32[8,512,128]{2,1,0:T(8,128)S(1)}, bf16[8,512,512]{2,1,0:T(8,128)(2,1)}, bf16[2048,512]{1,0:T(8,128)(2,1)}, ...), condition=%wide.region_2.3_spmd, body=%wide.region_1.2_spmd.sunk | while | flops 2688548864 | bytes 16515685 | solution.py:24
  114.9 3.1 fusion.48
  118.0 3.7 fusion.49
  121.7 3.1 fusion.48
  124.9 3.7 fusion.49
  128.6 3.1 fusion.48
  131.7 3.7 fusion.49
  135.4 3.1 fusion.48
  138.6 3.7 fusion.49
  142.3 3.1 fusion.48
  145.4 3.7 fusion.49
  149.1 3.1 fusion.48
  152.3 3.7 fusion.49
  156.0 3.1 fusion.48
  159.1 3.7 fusion.49
  162.8 3.1 fusion.48
  166.0 3.7 fusion.49
  169.7 1.3 copy-done.1
  171.0 60.5 %reduce-scatter.3.cloned.1.call-done = f32[256,128]{1,0:T(8,128)} async-done(((f32[4096,128]{1,0:T(8,128)}), f32[256,128]{1,0:T(8,128)}) %reduce-scatter.3.cloned.1.call-update) | async-done | bytes 131088 | tf_op jit(solution)/shard_map/reduce_scatter | solution.py:37
  232.5 68.0 %all-reduce.1 = (f32[128]{0:T(128)S(1)}, f32[128]{0:T(128)S(1)}) all-reduce(f32[128]{0:T(128)S(1)} %get-tuple-element.61, f32[128]{0:T(128)S(1)} %get-tuple-element.60), channel_id=1, replica_groups=mesh['row'=8,'col'=16] {'row','col'}, use_global_device_ids=true, to_apply=%region_7.8 | all-reduce | flops 256 | bytes 2048 | tf_op jit(solution)/shard_map/psum | solution.py:43
  302.7 1.1 fusion.28
  303.8 1.7 broadcast_divide_fusion
  305.8 41.2 %all-gather.8.cloned.1.call-done = f32[2048,128]{1,0:T(8,128)} async-done(((f32[256,128]{1,0:T(8,128)}), f32[2048,128]{1,0:T(8,128)}) %all-gather.8.cloned.1.call-update) | async-done | bytes 1048592 | tf_op jit(solution)/shard_map/all_gather | solution.py:36
  347.2 54.8 %while.21 = (s32[]{:T(128)}, f32[8,512,128]{2,1,0:T(8,128)S(1)}, bf16[8,512,512]{2,1,0:T(8,128)(2,1)}, bf16[2048,512]{1,0:T(8,128)(2,1)}, f32[2048,128]{1,0:T(8,128)}, /*index=5*/s32[]{:T(128)}) while((s32[]{:T(128)}, f32[8,512,128]{2,1,0:T(8,128)S(1)}, bf16[8,512,512]{2,1,0:T(8,128)(2,1)}, bf16[2048,512]{1,0:T(8,128)(2,1)}, ...), condition=%wide.region_12.13_spmd, body=%wide.region_11.12_spmd.sunk | while | flops 2688548864 | bytes 16515685 | solution.py:24
  347.2 3.1 fusion.53
  350.3 3.7 fusion.54
  354.1 3.1 fusion.53
  357.2 3.7 fusion.54
  360.9 3.1 fusion.53
  364.1 3.7 fusion.54
  367.8 3.1 fusion.53
  370.9 3.7 fusion.54
  374.6 3.1 fusion.53
  377.8 3.7 fusion.54
  381.5 3.1 fusion.53
  384.6 3.7 fusion.54
  388.3 3.1 fusion.53
  391.5 3.7 fusion.54
  395.2 3.1 fusion.53
  398.3 3.7 fusion.54
  402.0 1.3 copy-done
  403.4 62.6 %reduce-scatter.5.cloned.1.call-done = f32[256,128]{1,0:T(8,128)} async-done(((f32[4096,128]{1,0:T(8,128)}), f32[256,128]{1,0:T(8,128)}) %reduce-scatter.5.cloned.1.call-update) | async-done | bytes 131088 | tf_op jit(solution)/shard_map/reduce_scatter | solution.py:37
  467.1 67.5 %all-reduce = (f32[128]{0:T(128)S(1)}, f32[128]{0:T(128)S(1)}) all-reduce(f32[128]{0:T(128)S(1)} %get-tuple-element.59, f32[128]{0:T(128)S(1)} %get-tuple-element.58), channel_id=1, replica_groups=mesh['row'=8,'col'=16] {'row','col'}, use_global_device_ids=true, to_apply=%region_17.18 | all-reduce | flops 256 | bytes 2048 | tf_op jit(solution)/shard_map/psum | solution.py:43
  536.7 1.1 fusion.27
  (66 shorter events, 9.0 us)
Async XLA Ops:
  7.2 51.8 %all-gather.6.cloned.1.call-start = ((), (), s32[]{:S(2)}) async-start(), calls=%async_computation.3 | async-start | bytes 1179648 | tf_op jit(solution)/shard_map/all_gather | solution.py:36
  9.9 104.8 %all-gather.4.cloned.1.call-start = ((), (), s32[]{:S(2)}) async-start(), calls=%async_computation.2 | async-start | bytes 2359296 | tf_op jit(solution)/shard_map/all_gather | solution.py:31
  11.7 219.8 %reduce-scatter.3.cloned.1.call-start = ((), (), s32[]{:S(2)}) async-start(), calls=%async_computation.4 | async-start | bytes 2228224 | tf_op jit(solution)/shard_map/reduce_scatter | solution.py:37
  114.8 116.7 %copy-start.3 = (f32[256,128]{1,0:T(8,128)S(1)}, f32[256,128]{1,0:T(8,128)}, u32[]{:S(2)}) copy-start(f32[256,128]{1,0:T(8,128)} %param.7) | copy-start | bytes 393220
  114.8 3.1 copy-start.5
  121.7 3.1 copy-start.5
  128.6 3.1 copy-start.5
  135.4 3.1 copy-start.5
  142.3 3.1 copy-start.5
  149.1 3.1 copy-start.5
  156.0 3.1 copy-start.5
  162.8 3.1 copy-start.5
  169.7 1.3 copy-start.1
  171.0 176.0 %all-gather.8.cloned.1.call-start = ((), (), s32[]{:S(2)}) async-start(), calls=%async_computation.5 | async-start | bytes 1179648 | tf_op jit(solution)/shard_map/all_gather | solution.py:36
  305.6 160.4 %reduce-scatter.5.cloned.1.call-start = ((), (), s32[]{:S(2)}) async-start(), calls=%async_computation.6 | async-start | bytes 2228224 | tf_op jit(solution)/shard_map/reduce_scatter | solution.py:37
  347.2 118.8 %copy-start.2 = (f32[256,128]{1,0:T(8,128)S(1)}, f32[256,128]{1,0:T(8,128)}, u32[]{:S(2)}) copy-start(f32[256,128]{1,0:T(8,128)} %reduce-scatter.3.cloned.1.call-done) | copy-start | bytes 393220
  347.2 3.1 copy-start.6
  354.1 3.1 copy-start.6
  360.9 3.1 copy-start.6
  367.8 3.1 copy-start.6
  374.6 3.1 copy-start.6
  381.5 3.1 copy-start.6
  388.3 3.1 copy-start.6
  395.2 3.1 copy-start.6
  402.0 1.4 copy-start
  537.9 0.8 copy-start.4
Sparse Core Ops, SparseCore 0:
  10.9 48.0 all-gather.5
  61.3 53.3 all-gather.3
  171.1 60.3 reduce-scatter.2
  305.7 41.2 all-gather.7
  403.5 62.4 reduce-scatter.4
where the time goes:
time: 546 us; the launch traced here: 545 us
  waiting for transfers between devices  267 us (49%)
  blocking collectives  136 us (25%)
  matrix products  109 us (20%)
  between operations  13.9 us (3%)
  other arithmetic  13.8 us (3%)
    psum x2, blocking collectives, on_device(): lax.psum((jnp.sum(members, axis=0), jnp.sum(members * scores, axis=0)), (...  136 us
    reduce_scatter x2, waiting for transfers between devices, on_device(): lax.psum_scatter(kernel_product(features, column_panel, members_column),...  123 us
    all_gather x2, waiting for transfers between devices, on_device(): members_column = lax.all_gather(members, 'row', axis=0, tiled=True)  88.4 us
    dot_general x16, matrix products, block_product(): jnp.dot(kernel, members, precision=lax.Precision.HIGHEST, preferred_eleme...  58.9 us
    all_gather x1, waiting for transfers between devices, on_device(): column_panel = lax.all_gather(own_rows, 'row', axis=0, tiled=True)  55.7 us
    dot_general x16, matrix products, block_product(): jnp.einsum('bf,nf->bn', block, right_rows, preferred_element_type=jnp.flo...  50 us
  transfers between devices with their start and end apart: 5, of which 5 were waited for; matrix products, arithmetic and copies ran while one was open for 0% of the time, Pallas kernels for 0%

commit v1 on v0

--- a/solution.py
+++ b/solution.py
@@ -28,7 +28,15 @@
     frames = logits.shape[0]
     column = lax.axis_index("col")
     own_rows = lax.dynamic_slice_in_dim(features, column * frames, frames, 0)
-    column_panel = lax.all_gather(own_rows, "row", axis=0, tiled=True)
+    column_panel = jnp.concatenate(
+        lax.all_to_all(
+            jnp.stack(lax.axis_size("row") * [own_rows], axis=0),
+            axis_name="row",
+            split_axis=0,
+            concat_axis=0,
+        ),
+        axis=0,
+    )
     raised = jnp.exp(logits)
     members = raised / jnp.sum(raised, axis=1, keepdims=True)
     standardized = members

time: 546 us -> 505 us (0.925)
  waiting for transfers between devices: 267 us -> 220 us
  starting transfers between devices: 0.39 us -> 8.65 us
    all_gather x1 -> x0, waiting for transfers between devices: 55.7 us -> none  [on_device(): column_panel = lax.all_gather(own_rows, 'row', axis=0, tiled=True)]
    all_to_all x0 -> x1, waiting for transfers between devices: none -> 28 us  [on_device(): lax.all_to_all(jnp.stack(lax.axis_size('row') * [own_rows], axis=0), axis...]
    all_gather x2, waiting for transfers between devices: 88.4 us -> 66.9 us  [on_device(): members_column = lax.all_gather(members, 'row', axis=0, tiled=True)]
    all_to_all x0 -> x1, starting transfers between devices: none -> 8.31 us  [on_device(): lax.all_to_all(jnp.stack(lax.axis_size('row') * [own_rows], axis=0), axis...]
where the time goes in v1:
time: 505 us
  waiting for transfers between devices  220 us (44%)
  blocking collectives  135 us (27%)
  matrix products  109 us (22%)
  between operations  13.9 us (3%)
  other arithmetic  12 us (2%)
  starting transfers between devices  8.65 us (2%)
  local copies, waits for them, and re-layouts  5.53 us (1%)
    psum x2, blocking collectives, on_device(): lax.psum((jnp.sum(members, axis=0), jnp.sum(members * scores, axis=0)), (...  135 us
    reduce_scatter x2, waiting for transfers between devices, on_device(): lax.psum_scatter(kernel_product(features, column_panel, members_column),...  125 us
    all_gather x2, waiting for transfers between devices, on_device(): members_column = lax.all_gather(members, 'row', axis=0, tiled=True)  66.9 us
    dot_general x16, matrix products, block_product(): jnp.dot(kernel, members, precision=lax.Precision.HIGHEST, preferred_eleme...  58.9 us
    dot_general x16, matrix products, block_product(): jnp.einsum('bf,nf->bn', block, right_rows, preferred_element_type=jnp.flo...  50 us
    all_to_all x1, waiting for transfers between devices, on_device(): lax.all_to_all(jnp.stack(lax.axis_size('row') * [own_rows], axis=0), axis...  28 us
  transfers between devices with their start and end apart: 5, of which 5 were waited for; matrix products, arithmetic and copies ran while one was open for 0% of the time, Pallas kernels for 0%

profile of v1, /device:TPU:1, one launch (start us, length us, event | category | flops | bytes accessed | tf_op | source)
XLA Modules:
  0.0 505.0 jit_solution(4477725217365583627)
XLA Ops:
  8.2 1.5 stack.2
  9.7 8.3 %all-to-all-start = ((bf16[8,256,512]{2,1,0:T(8,128)(2,1)}), bf16[8,256,512]{2,1,0:T(8,128)(2,1)S(1)}, u32[]{:S(2)}, u32[]{:S(2)}) async-start(bf16[8,256,512]{2,1,0:T(8,128)(2,1)} %stack.2), calls=%async_computation | async-start | bytes 4194304 | tf_op jit(solution)/shard_map/all_to_all | solution.py:32
  19.0 28.0 %all-to-all-done = bf16[8,256,512]{2,1,0:T(8,128)(2,1)S(1)} async-done(((bf16[8,256,512]{2,1,0:T(8,128)(2,1)}), bf16[8,256,512]{2,1,0:T(8,128)(2,1)S(1)}, u32[]{:S(2)}, u32[]{:S(2)}) %all-to-all-start) | async-done | bytes 2097184 | tf_op jit(solution)/shard_map/all_to_all | solution.py:32
  47.0 25.8 %all-gather.3.cloned.1.call-done = f32[2048,128]{1,0:T(8,128)} async-done(((f32[256,128]{1,0:T(8,128)}), f32[2048,128]{1,0:T(8,128)}) %all-gather.3.cloned.1.call-update) | async-done | bytes 1048592 | tf_op jit(solution)/shard_map/all_gather | solution.py:44
  73.0 54.8 %while.20 = (s32[]{:T(128)}, f32[8,512,128]{2,1,0:T(8,128)S(1)}, bf16[8,512,512]{2,1,0:T(8,128)(2,1)}, bf16[2048,512]{1,0:T(8,128)(2,1)}, f32[2048,128]{1,0:T(8,128)}, /*index=5*/s32[]{:T(128)}) while((s32[]{:T(128)}, f32[8,512,128]{2,1,0:T(8,128)S(1)}, bf16[8,512,512]{2,1,0:T(8,128)(2,1)}, bf16[2048,512]{1,0:T(8,128)(2,1)}, ...), condition=%wide.region_2.3_spmd, body=%wide.region_1.2_spmd.sunk | while | flops 2688548864 | bytes 16515685 | solution.py:24
  73.0 3.1 fusion.48
  76.2 3.7 fusion.49
  79.9 3.1 fusion.48
  83.0 3.7 fusion.49
  86.7 3.1 fusion.48
  89.9 3.7 fusion.49
  93.6 3.1 fusion.48
  96.7 3.7 fusion.49
  100.4 3.1 fusion.48
  103.6 3.7 fusion.49
  107.3 3.1 fusion.48
  110.4 3.7 fusion.49
  114.1 3.1 fusion.48
  117.3 3.7 fusion.49
  121.0 3.1 fusion.48
  124.1 3.7 fusion.49
  127.8 1.3 copy-done.1
  129.2 62.5 %reduce-scatter.3.cloned.1.call-done = f32[256,128]{1,0:T(8,128)} async-done(((f32[4096,128]{1,0:T(8,128)}), f32[256,128]{1,0:T(8,128)}) %reduce-scatter.3.cloned.1.call-update) | async-done | bytes 131088 | tf_op jit(solution)/shard_map/reduce_scatter | solution.py:45
  192.8 67.7 %all-reduce.1 = (f32[128]{0:T(128)S(1)}, f32[128]{0:T(128)S(1)}) all-reduce(f32[128]{0:T(128)S(1)} %get-tuple-element.61, f32[128]{0:T(128)S(1)} %get-tuple-element.60), channel_id=1, replica_groups=mesh['row'=8,'col'=16] {'row','col'}, use_global_device_ids=true, to_apply=%region_7.8 | all-reduce | flops 256 | bytes 2048 | tf_op jit(solution)/shard_map/psum | solution.py:51
  262.6 1.1 fusion.28
  263.7 1.7 broadcast_divide_fusion
  265.7 41.1 %all-gather.5.cloned.1.call-done = f32[2048,128]{1,0:T(8,128)} async-done(((f32[256,128]{1,0:T(8,128)}), f32[2048,128]{1,0:T(8,128)}) %all-gather.5.cloned.1.call-update) | async-done | bytes 1048592 | tf_op jit(solution)/shard_map/all_gather | solution.py:44
  307.0 54.8 %while.21 = (s32[]{:T(128)}, f32[8,512,128]{2,1,0:T(8,128)S(1)}, bf16[8,512,512]{2,1,0:T(8,128)(2,1)}, bf16[2048,512]{1,0:T(8,128)(2,1)}, f32[2048,128]{1,0:T(8,128)}, /*index=5*/s32[]{:T(128)}) while((s32[]{:T(128)}, f32[8,512,128]{2,1,0:T(8,128)S(1)}, bf16[8,512,512]{2,1,0:T(8,128)(2,1)}, bf16[2048,512]{1,0:T(8,128)(2,1)}, ...), condition=%wide.region_12.13_spmd, body=%wide.region_11.12_spmd.sunk | while | flops 2688548864 | bytes 16515685 | solution.py:24
  307.0 3.1 fusion.53
  310.1 3.7 fusion.54
  313.9 3.1 fusion.53
  317.0 3.7 fusion.54
  320.7 3.1 fusion.53
  323.8 3.7 fusion.54
  327.6 3.1 fusion.53
  330.7 3.7 fusion.54
  334.4 3.1 fusion.53
  337.5 3.7 fusion.54
  341.3 3.1 fusion.53
  344.4 3.7 fusion.54
  348.1 3.1 fusion.53
  351.2 3.7 fusion.54
  355.0 3.1 fusion.53
  358.1 3.7 fusion.54
  361.8 1.3 copy-done
  363.2 62.5 %reduce-scatter.5.cloned.1.call-done = f32[256,128]{1,0:T(8,128)} async-done(((f32[4096,128]{1,0:T(8,128)}), f32[256,128]{1,0:T(8,128)}) %reduce-scatter.5.cloned.1.call-update) | async-done | bytes 131088 | tf_op jit(solution)/shard_map/reduce_scatter | solution.py:45
  426.8 67.7 %all-reduce = (f32[128]{0:T(128)S(1)}, f32[128]{0:T(128)S(1)}) all-reduce(f32[128]{0:T(128)S(1)} %get-tuple-element.59, f32[128]{0:T(128)S(1)} %get-tuple-element.58), channel_id=1, replica_groups=mesh['row'=8,'col'=16] {'row','col'}, use_global_device_ids=true, to_apply=%region_17.18 | all-reduce | flops 256 | bytes 2048 | tf_op jit(solution)/shard_map/psum | solution.py:51
  496.6 1.1 fusion.27
  (68 shorter events, 9.8 us)
Async XLA Ops:
  7.2 10.9 %copy-start.4 = (f32[256,128]{1,0:T(8,128)S(1)}, f32[256,128]{1,0:T(8,128)}, u32[]{:S(2)}) copy-start(f32[256,128]{1,0:T(8,128)} %param.7) | copy-start | bytes 393220
  9.7 37.3 %all-to-all-start = ((bf16[8,256,512]{2,1,0:T(8,128)(2,1)}), bf16[8,256,512]{2,1,0:T(8,128)(2,1)S(1)}, u32[]{:S(2)}, u32[]{:S(2)}) async-start(bf16[8,256,512]{2,1,0:T(8,128)(2,1)} %stack.2), calls=%async_computation | async-start | bytes 4194304 | tf_op jit(solution)/shard_map/all_to_all | solution.py:32
  18.0 54.8 %all-gather.3.cloned.1.call-start = ((), (), s32[]{:S(2)}) async-start(), calls=%async_computation.3 | async-start | bytes 1179648 | tf_op jit(solution)/shard_map/all_gather | solution.py:44
  19.0 172.7 %reduce-scatter.3.cloned.1.call-start = ((), (), s32[]{:S(2)}) async-start(), calls=%async_computation.4 | async-start | bytes 2228224 | tf_op jit(solution)/shard_map/reduce_scatter | solution.py:45
  47.0 25.8 %copy-start.3 = (bf16[8,256,512]{2,1,0:T(8,128)(2,1)}, bf16[8,256,512]{2,1,0:T(8,128)(2,1)S(1)}, u32[]{:S(2)}) copy-start(bf16[8,256,512]{2,1,0:T(8,128)(2,1)S(1)} %all-to-all-done) | copy-start | bytes 6291460
  73.0 3.1 copy-start.6
  79.9 3.1 copy-start.6
  86.7 3.1 copy-start.6
  93.6 3.1 copy-start.6
  100.4 3.1 copy-start.6
  107.3 3.1 copy-start.6
  114.1 3.1 copy-start.6
  121.0 3.1 copy-start.6
  127.8 1.3 copy-start.1
  129.1 177.7 %all-gather.5.cloned.1.call-start = ((), (), s32[]{:S(2)}) async-start(), calls=%async_computation.5 | async-start | bytes 1179648 | tf_op jit(solution)/shard_map/all_gather | solution.py:44
  265.5 160.2 %reduce-scatter.5.cloned.1.call-start = ((), (), s32[]{:S(2)}) async-start(), calls=%async_computation.6 | async-start | bytes 2228224 | tf_op jit(solution)/shard_map/reduce_scatter | solution.py:45
  307.0 118.7 %copy-start.2 = (f32[256,128]{1,0:T(8,128)S(1)}, f32[256,128]{1,0:T(8,128)}, u32[]{:S(2)}) copy-start(f32[256,128]{1,0:T(8,128)} %reduce-scatter.3.cloned.1.call-done) | copy-start | bytes 393220
  307.0 3.1 copy-start.7
  313.8 3.1 copy-start.7
  320.7 3.1 copy-start.7
  327.5 3.1 copy-start.7
  334.4 3.1 copy-start.7
  341.3 3.1 copy-start.7
  348.1 3.1 copy-start.7
  355.0 3.1 copy-start.7
  361.8 1.4 copy-start
  497.7 0.8 copy-start.5
Sparse Core Ops, SparseCore 0:
  21.8 51.0 all-gather.2
  129.3 62.4 reduce-scatter.2
  265.6 41.1 all-gather.4
  363.3 62.3 reduce-scatter.4
